TPU v7x, 32 devices: a whole 2x2x4 slice. The times are simulated.
32 devices in a mesh: seq: 2 (over y), dom: 8 (over z, x), tm: 2 (over core).
Axes of the slice: x: 2, y: 2, z: 4, core: 2. Of those that a mesh axis runs over, the one named last changes fastest.
Arguments:
- particles: bfloat16 [4, 1536, 128], P('tm', ('seq', 'dom')), parts along dimension 1, may hold values from -6 to 6
- log_weight: float32 [4, 1536], P('tm', ('seq', 'dom')), parts along dimension 1, may hold values from -13 to 313
- trans_weight: bfloat16 [128, 128], replicated, may hold values from -0.5 to 0.5
- precision: float32 [128], replicated, may hold values from 0.2 to 2
Outputs:
- smoothed: float32 [4, 1536], P('tm', ('seq', 'dom')), parts along dimension 1
- score: float32 [256, 128], P('seq'), parts along dimension 0
There are 2 independent parts, one for each index of `seq`. A program takes and returns all parts, laid end to end along the dimension named above; an argument that names none is the same for every part. Nothing has to cross between parts.
All inputs are finite; a program needn't handle non-finite values.
Results may differ from a plain program's by a relative error of at most 0.0061.
Values may be sent and summed in bfloat16 or wider, within the bound.
A program may use at most 64 MiB of HBM per device.

v0:
```python
import jax
import jax.numpy as jnp
from jax import lax
from jax.sharding import PartitionSpec as P

exact_mode = lax.Precision.HIGHEST


def from_behind(x, axis, by):
    size = lax.axis_size(axis)
    pairs = [(i, i + by) for i in range(size) if 0 <= i + by < size]
    return lax.ppermute(x, axis, pairs)


def block_size(length):
    best = 1
    for trial in range(1, min(length, 512) + 1):
        if length % trial == 0:
            best = trial
    return best


def project_rows(rows, precision, weight_full):
    return jnp.dot(rows.astype(jnp.float32) * precision, weight_full, precision=exact_mode).astype(
        jnp.bfloat16
    )


def pair_scores(row_proj, column_rows, column_bias):
    return (
        jnp.einsum("id,jd->ij", row_proj, column_rows, preferred_element_type=jnp.float32)
        + column_bias[None, :]
    )


def make_norm_fold(row_proj, bias_row, carried, block_in, first_row):
    length = block_in.shape[0]
    size = block_size(length)

    def inner(position, state):
        row_top, row_total = state
        offset = position * size
        column_rows = lax.dynamic_slice_in_dim(block_in, offset, size, 0)
        bias_part = lax.dynamic_slice_in_dim(bias_row, first_row + offset, size, 0)
        scores = pair_scores(row_proj, column_rows, bias_part)
        new_top = jnp.maximum(row_top, jnp.max(scores, axis=1))
        row_total = row_total * jnp.exp(row_top - new_top) + jnp.sum(
            jnp.exp(scores - new_top[:, None]), axis=1
        )
        return (new_top, row_total)

    return lax.fori_loop(0, length // size, inner, carried)


def make_column_fold(row_proj, bias_row, row_norm, row_weight, carried, block_in, first_row):
    length = block_in.shape[0]
    size = block_size(length)

    def inner(position, state):
        moved, column_sums = state
        offset = position * size
        column_rows = lax.dynamic_slice_in_dim(block_in, offset, size, 0)
        bias_part = lax.dynamic_slice_in_dim(bias_row, first_row + offset, size, 0)
        scores = pair_scores(row_proj, column_rows, bias_part)
        backward = (row_weight[:, None] * jnp.exp(scores - row_norm[:, None])).astype(jnp.bfloat16)
        moved = moved + jnp.dot(backward, column_rows, preferred_element_type=jnp.float32)
        column_sums = lax.dynamic_update_slice_in_dim(
            column_sums, jnp.sum(backward.astype(jnp.float32), axis=0), first_row + offset, 0
        )
        return (moved, column_sums)

    return lax.fori_loop(0, length // size, inner, carried)


def shards(particles, log_weight, trans_weight, precision):
    steps_here, rows_here, width = particles.shape
    tm_count = lax.axis_size("tm")
    dom_count = lax.axis_size("dom")
    total_rows = rows_here * dom_count
    tm_place = lax.axis_index("tm")
    is_last = tm_place == tm_count - 1
    weight_full = trans_weight.astype(jnp.float32)
    boundary = from_behind(particles[0], "tm", -1)
    later_sets = [particles[1]] + [boundary]
    later_proj = [project_rows(rows, precision, weight_full) for rows in later_sets]
    biases = []
    for k in range(steps_here):
        predicted = jnp.dot(particles[k], trans_weight.T, preferred_element_type=jnp.float32)
        biases.append(log_weight[k] - 0.5 * jnp.sum(precision * predicted * predicted, axis=1))
    local_bias = jnp.stack(biases)
    full_bias = lax.all_gather(local_bias, "dom", axis=1, tiled=True)
    row_norms = []
    whole = lax.all_gather(particles, "dom", axis=1, tiled=True)
    for k in range(steps_here):
        start_state = (
            jnp.full((rows_here,), -jnp.inf, jnp.float32),
            jnp.zeros((rows_here,), jnp.float32),
        )
        row_top, row_total = make_norm_fold(later_proj[k], full_bias[k], start_state, whole[k], 0)
        row_norms.append(row_top + jnp.log(row_total))
    final_logs = log_weight[steps_here - 1]
    global_top = lax.pmax(jnp.max(final_logs), "dom")
    global_total = lax.psum(jnp.sum(jnp.exp(final_logs - global_top)), "dom")
    final_weights = jnp.exp(final_logs - global_top) / global_total
    carried = (
        jnp.zeros((steps_here, rows_here), jnp.float32),
        jnp.zeros((width, width), jnp.float32),
    )
    for r in range(tm_count):
        if r == 0:
            incoming = jnp.zeros((rows_here,), jnp.float32)
        else:
            incoming = from_behind(carried[0][0], "tm", -1)
        owner = tm_count - 1 - r
        backward_partial_value = jnp.zeros((width, width), jnp.float32)
        outputs = [None] * steps_here
        row_weight = incoming
        for backward_k in range(steps_here - 1, -1, -1):
            column_rows = particles[backward_k]
            backward_start_state = (
                jnp.zeros((rows_here, width), jnp.float32),
                jnp.zeros((total_rows,), jnp.float32),
            )
            moved, column_sums = make_column_fold(
                later_proj[backward_k],
                full_bias[backward_k],
                row_norms[backward_k],
                row_weight,
                backward_start_state,
                whole[backward_k],
                0,
            )
            column_weights = lax.psum_scatter(column_sums, "dom", scatter_dimension=0, tiled=True)
            outer = jnp.dot(
                later_sets[backward_k].astype(jnp.float32).T, moved, precision=exact_mode
            )
            column_float = column_rows.astype(jnp.float32)
            moment = jnp.dot(
                column_float.T * column_weights[None, :], column_float, precision=exact_mode
            )
            backward_partial_value = backward_partial_value + precision[:, None] * (
                outer - jnp.dot(weight_full, moment, precision=exact_mode)
            )
            if backward_k == steps_here - 1:
                column_weights = jnp.where(is_last, final_weights, column_weights)
            outputs[backward_k] = column_weights
            row_weight = column_weights
        is_owner = tm_place == owner
        carried = (
            jnp.where(is_owner, jnp.stack(outputs), carried[0]),
            jnp.where(is_owner, backward_partial_value, carried[1]),
        )
    stacked, partial_value = carried
    score = lax.psum(partial_value, ("dom", "tm"))
    return (stacked * total_rows, score)


def solution(mesh):
    placed = (P("tm", ("seq", "dom"), None), P("tm", ("seq", "dom")), P(), P())
    return jax.shard_map(
        shards,
        mesh=mesh,
        in_specs=placed,
        out_specs=(P("tm", ("seq", "dom")), P("seq", None)),
        check_vma=False,
    )
```

profile of v0, /device:TPU:8, one launch (start us, length us, event | category | flops | bytes accessed | tf_op | source)
XLA Modules:
  0.0 267.3 jit_solution(9784451875654501515)
XLA Ops:
  7.2 0.8 slice_bitcast_fusion.2
  8.0 1.4 collective-permute-start
  9.4 28.6 %all_gather.6 = bf16[2,768,128]{2,1,0:T(8,128)(2,1)S(1)} all-gather(bf16[2,96,128]{2,1,0:T(8,128)(2,1)S(1)} %copy-done.1), channel_id=1, replica_groups=mesh['seq'=2,'dom'=8,'tm'=2] {'dom'}, dimensions={1}, use_global_device_ids=true | all-gather | bytes 442368 | tf_op jit(solution)/shard_map/all_gather | solution.py:93
  38.0 0.3 fusion.54
  38.3 0.3 fusion.53
  38.8 0.6 copy-done.3
  39.4 0.6 slice_reduce_fusion.2
  40.0 22.1 %pmax.7 = f32[]{:T(128)} all-reduce(f32[]{:T(128)} %slice_reduce_fusion.2), channel_id=1, replica_groups=mesh['seq'=2,'dom'=8,'tm'=2] {'dom'}, use_global_device_ids=true, to_apply=%region_3.4 | all-reduce | flops 1 | bytes 8 | tf_op jit(solution)/shard_map/pmax | solution.py:102
  62.1 1.2 fusion.81
  63.3 16.3 %all-gather = f32[8,96,2]{1,2,0:T(2,128)S(1)} all-gather(f32[1,96,2]{1,2,0:T(2,128)S(1)} %maximum_bitcast_fusion), channel_id=1, replica_groups=mesh['seq'=2,'dom'=8,'tm'=2] {'dom'}, dimensions={0}, use_global_device_ids=true | all-gather | bytes 6912 | tf_op jit(solution)/shard_map/all_gather | solution.py:91
  79.7 1.2 while.98
  79.8 0.3 fusion.143
  80.4 0.3 fusion.143
  81.0 0.6 copy-done.4
  81.7 0.6 dynamic-slice
  83.1 1.2 while.96
  83.2 0.3 fusion.136
  83.7 0.3 fusion.136
  84.3 1.5 while.97
  84.8 0.2 dynamic_update_slice.36
  85.5 0.2 dynamic_update_slice.36
  85.8 19.9 %all-reduce.4 = (f32[768]{0:T(1024)S(1)}, f32[]{:T(128)}) all-reduce(f32[768]{0:T(1024)S(1)} %get-tuple-element.769, f32[]{:T(128)} %get-tuple-element.1041), channel_id=2, replica_groups=mesh['seq'=2,'dom'=8,'tm'=2] {'dom'}, use_global_device_ids=true, to_apply=%region_13.0.clone | all-reduce | flops 769 | bytes 6152
  105.6 1.3 broadcast_select_fusion.5
  106.9 1.5 while.99
  107.4 0.2 dynamic_update_slice.37
  108.1 0.2 dynamic_update_slice.37
  108.4 17.1 %all-reduce.1 = f32[768]{0:T(1024)S(1)} all-reduce(f32[768]{0:T(1024)S(1)} %get-tuple-element.772), channel_id=3, replica_groups=mesh['seq'=2,'dom'=8,'tm'=2] {'dom'}, use_global_device_ids=true, to_apply=%region_21.22.clone | all-reduce | flops 768 | bytes 6144
  125.6 1.3 collective-permute-start.1
  127.2 0.3 fusion.52
  127.5 0.3 fusion.50
  127.8 0.2 fusion.86
  128.1 0.2 convolution_subtract_fusion
  128.3 0.3 fusion.44
  128.7 1.5 while.100
  129.1 0.2 dynamic_update_slice.38
  129.9 0.2 dynamic_update_slice.38
  130.1 19.1 %all-reduce.2 = f32[768]{0:T(1024)S(1)} all-reduce(f32[768]{0:T(1024)S(1)} %get-tuple-element.773), channel_id=4, replica_groups=mesh['seq'=2,'dom'=8,'tm'=2] {'dom'}, use_global_device_ids=true, to_apply=%region_25.26.clone | all-reduce | flops 768 | bytes 6144
  149.3 1.5 while.101
  149.8 0.2 dynamic_update_slice.39
  150.5 0.2 dynamic_update_slice.39
  150.8 17.1 %all-reduce.3 = f32[768]{0:T(1024)S(1)} all-reduce(f32[768]{0:T(1024)S(1)} %get-tuple-element.774), channel_id=5, replica_groups=mesh['seq'=2,'dom'=8,'tm'=2] {'dom'}, use_global_device_ids=true, to_apply=%region_29.30.clone | all-reduce | flops 768 | bytes 6144
  168.3 0.3 fusion.51
  168.6 0.3 fusion.49
  169.2 0.2 convolution_subtract_fusion.2
  169.4 0.9 fusion.48
  170.4 0.6 fusion.80
  170.9 88.0 %all-reduce.7.cloned.1.call-done = f32[128,128]{0,1:T(8,128)} async-done(((f32[128,128]{0,1:T(8,128)}), f32[128,128]{0,1:T(8,128)}) %all-reduce.7.cloned.1.call-update) | async-done | bytes 65552 | tf_op jit(solution)/shard_map/psum | solution.py:154
  258.9 1.6 copy.10
  (86 shorter events, 6.6 us)
Async XLA Ops:
  7.2 30.9 %copy-start = (bf16[128,128]{1,0:T(8,128)(2,1)S(1)}, bf16[128,128]{1,0:T(8,128)(2,1)}, u32[]{:S(2)}) copy-start(bf16[128,128]{1,0:T(8,128)(2,1)} %param.18) | copy-start | bytes 98308
  7.2 2.2 copy-start.1
  7.2 251.7 %all-reduce.7.cloned.1.call-start = ((), (), s32[]{:S(2)}) async-start(), calls=%async_computation | async-start | bytes 131072 | tf_op jit(solution)/shard_map/psum | solution.py:154
  8.0 30.0 %copy-start.2 = (f32[128]{0:T(128)S(1)}, f32[128]{0:T(128)}, u32[]{:S(2)}) copy-start(f32[128]{0:T(128)} %param.19) | copy-start | bytes 1540
  8.0 74.9 %collective-permute-start = (bf16[96,128]{1,0:T(8,128)(2,1)S(1)}, bf16[96,128]{1,0:T(8,128)(2,1)S(1)}, u32[]{:S(2)}, u32[]{:S(2)}) collective-permute-start(bf16[96,128]{1,0:T(8,128)(2,1)S(1)} %slice_bitcast_fusion.2), channel_id=1, source_target_pairs={{1,0},{3,2},{5,4},{7,6},{9,8},{11,10},{13,12},{15,14},{17,16},{19,... | collective-permute-start | bytes 73736 | tf_op jit(solution)/shard_map/ppermute | solution.py:12
  38.7 0.7 copy-start.3
  81.0 0.7 copy-start.4
  125.6 3.0 %collective-permute-start.1 = (f32[96]{0:T(128)S(1)}, f32[96]{0:T(128)S(1)}, u32[]{:S(2)}, u32[]{:S(2)}) collective-permute-start(f32[96]{0:T(128)S(1)} %slice_bitcast_fusion.3), channel_id=1, source_target_pairs={{1,0},{3,2},{5,4},{7,6},{9,8},{11,10},{13,12},{15,14},{17,16},{19,... | collective-permute-start | bytes 1160 | tf_op jit(solution)/shard_map/ppermute | solution.py:12
Sparse Core Ops, SparseCore 0:
  170.5 88.4 all-reduce.6
where the time goes:
time: 268 us; the launch traced here: 267 us
  blocking collectives  140 us (52%)
  waiting for transfers between devices  88.1 us (33%)
  between operations  14.9 us (6%)
  matrix products  8.92 us (3%)
  local copies, waits for them, and re-layouts  7.58 us (3%)
  other arithmetic  4.58 us (2%)
  starting transfers between devices  2.74 us (1%)
    psum x1, waiting for transfers between devices, shards(): score = lax.psum(partial_value, ('dom', 'tm'))  88 us
    unnamed x4, blocking collectives  73.2 us
    all_gather x1, blocking collectives, shards(): whole = lax.all_gather(particles, 'dom', axis=1, tiled=True)  28.6 us
    pmax x1, blocking collectives, shards(): global_top = lax.pmax(jnp.max(final_logs), 'dom')  22.1 us
    all_gather x1, blocking collectives, shards(): full_bias = lax.all_gather(local_bias, 'dom', axis=1, tiled=True)  16.3 us
  transfers between devices with their start and end apart: 3, of which 2 were waited for; matrix products, arithmetic and copies ran while one was open for 2% of the time, Pallas kernels for 0%

commit v1 on v0

--- a/solution.py
+++ b/solution.py
@@ -151,7 +151,7 @@
             jnp.where(is_owner, backward_partial_value, carried[1]),
         )
     stacked, partial_value = carried
-    score = lax.psum(partial_value, ("dom", "tm"))
+    score = jnp.sum(lax.all_gather(partial_value, ("dom", "tm")), axis=0)
     return (stacked * total_rows, score)
 
 

time: 268 us -> 220 us (0.82)
  waiting for transfers between devices: 88.1 us -> 37.9 us
    psum x1 -> x0, waiting for transfers between devices: 88 us -> none  [shards(): score = lax.psum(partial_value, ('dom', 'tm'))]
    all_gather x0 -> x1, waiting for transfers between devices: none -> 37.8 us  [shards(): score = jnp.sum(lax.all_gather(partial_value, ('dom', 'tm')), axis=0)]
  transfers between devices with their start and end apart: 3 -> 3, of which waited for: 2 -> 2; matrix products, arithmetic and copies ran while one was open for 2% -> 3% of each run, Pallas kernels for 0% -> 0%
where the time goes in v1:
time: 220 us; the launch traced here: 218 us
  blocking collectives  140 us (64%)
  waiting for transfers between devices  37.9 us (17%)
  between operations  15 us (7%)
  matrix products  9.59 us (4%)
  local copies, waits for them, and re-layouts  7.52 us (3%)
  other arithmetic  4.81 us (2%)
  starting transfers between devices  2.74 us (1%)
    unnamed x4, blocking collectives  73.2 us
    all_gather x1, waiting for transfers between devices, shards(): score = jnp.sum(lax.all_gather(partial_value, ('dom', 'tm')), axis=0)  37.8 us
    all_gather x1, blocking collectives, shards(): whole = lax.all_gather(particles, 'dom', axis=1, tiled=True)  28.6 us
    pmax x1, blocking collectives, shards(): global_top = lax.pmax(jnp.max(final_logs), 'dom')  22.1 us
    all_gather x1, blocking collectives, shards(): full_bias = lax.all_gather(local_bias, 'dom', axis=1, tiled=True)  16.3 us
  transfers between devices with their start and end apart: 3, of which 2 were waited for; matrix products, arithmetic and copies ran while one was open for 3% of the time, Pallas kernels for 0%

profile of v1, /device:TPU:8, one launch (start us, length us, event | category | flops | bytes accessed | tf_op | source)
XLA Modules:
  0.0 218.0 jit_solution(16915847375850644225)
XLA Ops:
  7.2 0.8 slice_bitcast_fusion.2
  8.0 1.4 collective-permute-start
  9.4 0.9 fusion.53
  10.4 0.3 fusion.54
  10.8 28.6 %all_gather.12 = bf16[2,768,128]{2,1,0:T(8,128)(2,1)S(1)} all-gather(bf16[2,96,128]{2,1,0:T(8,128)(2,1)S(1)} %copy-done.1), channel_id=1, replica_groups=mesh['seq'=2,'dom'=8,'tm'=2] {'dom'}, dimensions={1}, use_global_device_ids=true | all-gather | bytes 442368 | tf_op jit(solution)/shard_map/all_gather | solution.py:93
  39.4 0.6 slice_reduce_fusion.2
  40.0 22.1 %pmax.7 = f32[]{:T(128)} all-reduce(f32[]{:T(128)} %slice_reduce_fusion.2), channel_id=1, replica_groups=mesh['seq'=2,'dom'=8,'tm'=2] {'dom'}, use_global_device_ids=true, to_apply=%region_3.4 | all-reduce | flops 1 | bytes 8 | tf_op jit(solution)/shard_map/pmax | solution.py:102
  62.1 1.2 fusion.81
  63.4 16.3 %all-gather.1 = f32[8,96,2]{1,2,0:T(2,128)S(1)} all-gather(f32[1,96,2]{1,2,0:T(2,128)S(1)} %maximum_bitcast_fusion), channel_id=1, replica_groups=mesh['seq'=2,'dom'=8,'tm'=2] {'dom'}, dimensions={0}, use_global_device_ids=true | all-gather | bytes 6912 | tf_op jit(solution)/shard_map/all_gather | solution.py:91
  79.8 1.2 while.98
  79.9 0.3 fusion.143
  80.5 0.3 fusion.143
  81.1 0.6 copy-done.4
  81.7 0.6 dynamic-slice
  83.1 1.2 while.96
  83.2 0.3 fusion.136
  83.8 0.3 fusion.136
  84.4 1.5 while.97
  84.9 0.2 dynamic_update_slice.36
  85.6 0.2 dynamic_update_slice.36
  85.8 19.9 %all-reduce.4 = (f32[768]{0:T(1024)S(1)}, f32[]{:T(128)}) all-reduce(f32[768]{0:T(1024)S(1)} %get-tuple-element.769, f32[]{:T(128)} %get-tuple-element.1037), channel_id=3, replica_groups=mesh['seq'=2,'dom'=8,'tm'=2] {'dom'}, use_global_device_ids=true, to_apply=%region_13.0.clone | all-reduce | flops 769 | bytes 6152
  105.7 1.3 broadcast_select_fusion.5
  107.0 1.5 while.99
  107.5 0.2 dynamic_update_slice.37
  108.2 0.2 dynamic_update_slice.37
  108.4 17.1 %all-reduce.1 = f32[768]{0:T(1024)S(1)} all-reduce(f32[768]{0:T(1024)S(1)} %get-tuple-element.772), channel_id=4, replica_groups=mesh['seq'=2,'dom'=8,'tm'=2] {'dom'}, use_global_device_ids=true, to_apply=%region_21.22.clone | all-reduce | flops 768 | bytes 6144
  125.7 1.3 collective-permute-start.1
  127.0 0.3 fusion.52
  127.6 0.3 fusion.50
  127.9 0.2 fusion.86
  128.2 0.2 convolution_subtract_fusion
  128.4 0.3 fusion.44
  128.7 1.5 while.100
  129.2 0.2 dynamic_update_slice.38
  129.9 0.2 dynamic_update_slice.38
  130.2 19.1 %all-reduce.2 = f32[768]{0:T(1024)S(1)} all-reduce(f32[768]{0:T(1024)S(1)} %get-tuple-element.773), channel_id=5, replica_groups=mesh['seq'=2,'dom'=8,'tm'=2] {'dom'}, use_global_device_ids=true, to_apply=%region_25.26.clone | all-reduce | flops 768 | bytes 6144
  149.4 1.5 while.101
  149.9 0.2 dynamic_update_slice.39
  150.6 0.2 dynamic_update_slice.39
  150.8 17.1 %all-reduce.3 = f32[768]{0:T(1024)S(1)} all-reduce(f32[768]{0:T(1024)S(1)} %get-tuple-element.774), channel_id=6, replica_groups=mesh['seq'=2,'dom'=8,'tm'=2] {'dom'}, use_global_device_ids=true, to_apply=%region_29.30.clone | all-reduce | flops 768 | bytes 6144
  168.0 0.3 fusion.51
  168.4 0.3 fusion.49
  169.2 0.2 convolution_subtract_fusion.2
  169.4 0.9 fusion.48
  170.4 0.6 fusion.80
  171.0 37.8 %all-gather.4.cloned.1.call-done = f32[2048,128]{0,1:T(8,128)} async-done(((f32[128,128]{0,1:T(8,128)}), f32[2048,128]{0,1:T(8,128)}) %all-gather.4.cloned.1.call-update) | async-done | bytes 1048592 | tf_op jit(solution)/shard_map/all_gather | solution.py:154
  208.8 1.4 copy.9
  210.4 0.7 copy.8
  (88 shorter events, 6.8 us)
Async XLA Ops:
  7.2 2.3 %copy-start = (bf16[128,128]{1,0:T(8,128)(2,1)S(1)}, bf16[128,128]{1,0:T(8,128)(2,1)}, u32[]{:S(2)}) copy-start(bf16[128,128]{1,0:T(8,128)(2,1)} %param.18) | copy-start | bytes 98308
  7.2 2.2 %copy-start.1 = (bf16[2,96,128]{2,1,0:T(8,128)(2,1)S(1)}, bf16[2,96,128]{2,1,0:T(8,128)(2,1)}, u32[]{:S(2)}) copy-start(bf16[2,96,128]{2,1,0:T(8,128)(2,1)} %param.16) | copy-start | bytes 147460
  7.2 201.6 %all-gather.4.cloned.1.call-start = ((), (), s32[]{:S(2)}) async-start(), calls=%async_computation | async-start | bytes 1114112 | tf_op jit(solution)/shard_map/all_gather | solution.py:154
  8.0 2.4 %copy-start.2 = (f32[128]{0:T(128)S(1)}, f32[128]{0:T(128)}, u32[]{:S(2)}) copy-start(f32[128]{0:T(128)} %param.19) | copy-start | bytes 1540
  8.0 75.0 %collective-permute-start = (bf16[96,128]{1,0:T(8,128)(2,1)S(1)}, bf16[96,128]{1,0:T(8,128)(2,1)S(1)}, u32[]{:S(2)}, u32[]{:S(2)}) collective-permute-start(bf16[96,128]{1,0:T(8,128)(2,1)S(1)} %slice_bitcast_fusion.2), channel_id=1, source_target_pairs={{1,0},{3,2},{5,4},{7,6},{9,8},{11,10},{13,12},{15,14},{17,16},{19,... | collective-permute-start | bytes 73736 | tf_op jit(solution)/shard_map/ppermute | solution.py:12
  10.8 28.6 %copy-start.3 = (f32[2,96]{1,0:T(2,128)S(1)}, f32[2,96]{1,0:T(2,128)}, u32[]{:S(2)}) copy-start(f32[2,96]{1,0:T(2,128)} %param.17) | copy-start | bytes 2308
  81.1 0.7 copy-start.4
  125.7 3.0 %collective-permute-start.1 = (f32[96]{0:T(128)S(1)}, f32[96]{0:T(128)S(1)}, u32[]{:S(2)}, u32[]{:S(2)}) collective-permute-start(f32[96]{0:T(128)S(1)} %slice_bitcast_fusion.3), channel_id=1, source_target_pairs={{1,0},{3,2},{5,4},{7,6},{9,8},{11,10},{13,12},{15,14},{17,16},{19,... | collective-permute-start | bytes 1160 | tf_op jit(solution)/shard_map/ppermute | solution.py:12
Sparse Core Ops, SparseCore 0:
  170.5 38.3 all-gather.3
